TPU v7x, 256 devices: a whole 4x4x8 slice. The times are simulated.
256 devices in a mesh: dp: 16 (over z, core), tensor: 4 (over y), corpus: 4 (over x).
Axes of the slice: x: 4, y: 4, z: 8, core: 2. Of those that a mesh axis runs over, the one named last changes fastest.
Arguments:
- queries: bfloat16 [4096, 2048], P(('dp', 'tensor', 'corpus')), may hold values from -24 to 24
- passages: bfloat16 [65536, 2048], P(('dp', 'corpus'), 'tensor'), may hold values from -6 to 6
- pos_ids: int32 [4096], P(('dp', 'tensor', 'corpus')), may hold values from 0 to 65535, as said below
- neg_ids: int32 [4096, 32], P(('dp', 'tensor', 'corpus')), may hold values from 0 to 65535, as said below
Outputs:
- grad_query: float32 [4096, 2048], P(('dp', 'tensor', 'corpus'))
- losses: float32 [4096], P(('dp', 'tensor', 'corpus'))
- grad_pass: float32 [65536, 2048], P(('dp', 'corpus'), 'tensor')
Inputs may be any that keep to these rules, and one draw needn't show every extreme that they name: `pos_ids`: together with neg_ids: the ids named by the 16 queries of one device, positives and negatives together, fall at most 16 times into one block of 1024 passage rows (rows b * 1024 to (b + 1) * 1024 - 1), and exactly 16 times into one block that is the same for every device. Ids may repeat. `neg_ids`: counted together with pos_ids as stated there.
All inputs are finite; a program needn't handle non-finite values.
Results may differ from a plain program's by a relative error of at most 0.0035.
Values may be sent and summed in bfloat16 or wider, within the bound.
A program may use at most 128 MiB of HBM per device.

v0:
```python
import jax
import jax.numpy as jnp
from jax import lax
from jax.sharding import PartitionSpec as P


def lookup_rows(row_table, asked_ids):
    return jnp.take(row_table, asked_ids, axis=0, mode="fill", fill_value=0)


def body(queries, passages, pos_ids, neg_ids):
    per_device, feat_width = queries.shape
    block_rows, shard_width = passages.shape
    neg_count = neg_ids.shape[1]
    owners = lax.axis_size("dp") * lax.axis_size("corpus")
    slot_count = 2 * per_device * (neg_count + 1) // owners
    score_scale = feat_width ** (-0.5)
    wanted = jnp.concatenate([pos_ids[:, None], neg_ids], axis=1).reshape(-1)
    owner_of = wanted // block_rows
    local_row = wanted % block_rows
    matches = (owner_of[:, None] == jnp.arange(owners)[None, :]).astype(jnp.int32)
    earlier = jnp.cumsum(matches, axis=0) - matches
    slot_of = owner_of * slot_count + jnp.sum(earlier * matches, axis=1)
    send_ids = jnp.full((owners * slot_count,), block_rows, jnp.int32).at[slot_of].set(local_row)
    send_ids = send_ids.reshape(owners, slot_count)
    row_table = lax.all_gather(passages, "tensor", axis=1, tiled=True)
    asked_ids = lax.all_to_all(send_ids, ("dp", "corpus"), split_axis=0, concat_axis=0, tiled=True)
    found = lookup_rows(row_table, asked_ids)
    fetched = lax.all_to_all(found, ("dp", "corpus"), split_axis=0, concat_axis=0, tiled=True)
    gathered = fetched.reshape(owners * slot_count, feat_width)[slot_of]
    gathered = gathered.reshape(per_device, neg_count + 1, feat_width)
    pos_rows = gathered[:, 0, :]
    neg_rows = gathered[:, 1:, :]
    in_batch = lax.all_gather(pos_rows, "dp", axis=0, tiled=True)
    columns = in_batch.shape[0]
    in_scores = (
        lax.dot_general(
            queries, in_batch, (((1,), (1,)), ((), ())), preferred_element_type=jnp.float32
        )
        * score_scale
    )
    neg_scores = (
        jnp.einsum("md,mkd->mk", queries, neg_rows, preferred_element_type=jnp.float32)
        * score_scale
    )
    logits = jnp.concatenate([in_scores, neg_scores], axis=1)
    row_max = jnp.max(logits, axis=1, keepdims=True)
    exponent = jnp.exp(logits - row_max)
    denominator = jnp.sum(exponent, axis=1, keepdims=True)
    own_col = lax.axis_index("dp") * per_device + jnp.arange(per_device)
    target = (jnp.arange(columns + neg_count)[None, :] == own_col[:, None]).astype(jnp.float32)
    losses = jnp.log(denominator[:, 0]) + row_max[:, 0] - jnp.sum(target * logits, axis=1)
    weights = (exponent / denominator - target).astype(jnp.bfloat16)
    in_weights = weights[:, :columns]
    neg_weights = weights[:, columns:]
    grad_query = jnp.dot(in_weights, in_batch, preferred_element_type=jnp.float32)
    grad_query = grad_query + jnp.einsum(
        "mk,mkd->md", neg_weights, neg_rows, preferred_element_type=jnp.float32
    )
    grad_query = grad_query * score_scale
    in_terms = lax.dot_general(
        in_weights, queries, (((0,), (0,)), ((), ())), preferred_element_type=jnp.float32
    )
    pos_grad = lax.psum_scatter(in_terms, "dp", scatter_dimension=0, tiled=True) * score_scale
    neg_grad = (
        neg_weights.astype(jnp.float32)[:, :, None]
        * queries.astype(jnp.float32)[:, None, :]
        * score_scale
    )
    row_grads = jnp.concatenate([pos_grad[:, None, :], neg_grad], axis=1).astype(jnp.bfloat16)
    row_grads = row_grads.reshape(-1, feat_width)
    grad_slots = (
        jnp.zeros((owners * slot_count, feat_width), jnp.bfloat16).at[slot_of].set(row_grads)
    )
    grad_slots = grad_slots.reshape(owners, slot_count, feat_width)
    arrived = lax.all_to_all(grad_slots, ("dp", "corpus"), split_axis=0, concat_axis=0, tiled=True)
    accum_grad = jnp.zeros((block_rows, feat_width), jnp.float32)
    accum_grad = accum_grad.at[asked_ids.reshape(-1)].add(
        arrived.reshape(-1, feat_width).astype(jnp.float32), mode="drop"
    )
    grad_pass = lax.psum_scatter(accum_grad, "tensor", scatter_dimension=1, tiled=True)
    return (grad_query, losses, grad_pass)


def solution(mesh):
    in_specs = (
        P(("dp", "tensor", "corpus"), None),
        P(("dp", "corpus"), "tensor"),
        P(("dp", "tensor", "corpus")),
        P(("dp", "tensor", "corpus"), None),
    )
    out_specs = (
        P(("dp", "tensor", "corpus"), None),
        P(("dp", "tensor", "corpus")),
        P(("dp", "corpus"), "tensor"),
    )
    return jax.shard_map(body, mesh=mesh, in_specs=in_specs, out_specs=out_specs, check_vma=False)
```

profile of v0, /device:TPU:1, one launch (start us, length us, event | category | flops | bytes accessed | tf_op | source)
XLA Modules:
  0.0 520.4 jit_solution(17081883421997860384)
XLA Ops:
  7.2 0.7 all-gather.4.cloned.1.call-update
  7.9 0.7 copy.13
  8.6 0.8 pad_add_fusion
  9.7 1.5 reduce-window.6
  11.7 4.1 scatter_custom_fusion
  15.8 22.0 %all_to_all.25 = s32[64,1,16]{2,1,0:T(1,128)S(1)} all-to-all(s32[64,1,16]{2,1,0:T(1,128)S(1)} %bitcast.53), channel_id=1, replica_groups=mesh['dp'=16,'tensor'=4,'corpus'=4] {'dp','corpus'}, dimensions={0} | all-to-all | bytes 8192 | tf_op jit(solution)/shard_map/all_to_all | solution.py:27
  37.9 26.3 %all-gather.4.cloned.1.call-done = bf16[1024,2048]{1,0:T(8,128)(2,1)} async-done(((bf16[1024,512]{1,0:T(8,128)(2,1)}), bf16[1024,2048]{1,0:T(8,128)(2,1)}) %all-gather.4.cloned.1.call-update) | async-done | bytes 4194320 | tf_op jit(solution)/shard_map/all_gather | solution.py:26
  64.2 11.6 %gather_fusion = bf16[1024,2048]{1,0:T(8,128)(2,1)} fusion(bf16[1024,2048]{1,0:T(8,128)(2,1)} %all-gather.4.cloned.1.call-done, s32[1024]{0:T(1024)S(1)} %broadcast_clamp_fusion), kind=kCustom, calls=%fused_computation | custom fusion | bytes 8392704 | tf_op jit(solution)/shard_map/jit(_take)/gather | solution.py:8
  75.8 4.5 broadcast_select_fusion
  80.3 11.0 %all-to-all-start.1 = ((bf16[64,16,2048]{2,1,0:T(8,128)(2,1)}), bf16[64,16,2048]{2,1,0:T(8,128)(2,1)}, u32[]{:S(2)}, u32[]{:S(2)}) async-start(bf16[64,16,2048]{2,1,0:T(8,128)(2,1)} %broadcast_select_fusion), calls=%async_computation.1 | async-start | bytes 8388608 | tf_op jit(solution)/shard_map/all_to_all | solution.py:29
  91.4 93.5 %all-to-all-done.1 = bf16[64,16,2048]{2,1,0:T(8,128)(2,1)} async-done(((bf16[64,16,2048]{2,1,0:T(8,128)(2,1)}), bf16[64,16,2048]{2,1,0:T(8,128)(2,1)}, u32[]{:S(2)}, u32[]{:S(2)}) %all-to-all-start.1) | async-done | bytes 4194336 | tf_op jit(solution)/shard_map/all_to_all | solution.py:29
  184.9 9.0 %gather_fusion.1 = bf16[528,2048]{1,0:T(8,128)(2,1)S(1)} fusion(bf16[1024,2048]{1,0:T(8,128)(2,1)} %bitcast.6, s32[1024]{0:T(1024)S(1)} %pad_clamp_fusion), kind=kCustom, calls=%fused_computation.1 | custom fusion | bytes 4327488 | tf_op jit(solution)/shard_map/gather | solution.py:30
  193.9 1.9 reshape.222
  195.8 1.1 slice.34
  196.9 0.7 copy.17
  197.8 2.4 fusion.8
  200.4 34.0 %all-gather.6.cloned.1.call-done = bf16[256,1,2048]{2,0,1:T(8,128)(2,1)} async-done(((bf16[16,1,2048]{2,0,1:T(8,128)(2,1)}), bf16[256,1,2048]{2,0,1:T(8,128)(2,1)}) %all-gather.6.cloned.1.call-update) | async-done | bytes 1048592 | tf_op jit(solution)/shard_map/all_gather | solution.py:34
  234.4 1.7 fusion.27
  236.4 1.8 fusion.18
  238.2 1.8 multiply_convert_fusion
  240.1 53.7 %reduce-scatter.3.cloned.1.call-done = f32[16,2048]{1,0:T(8,128)} async-done(((f32[256,2048]{1,0:T(8,128)}), f32[16,2048]{1,0:T(8,128)}) %reduce-scatter.3.cloned.1.call-update) | async-done | bytes 131088 | tf_op jit(solution)/shard_map/reduce_scatter | solution.py:64
  293.8 0.9 fusion.15
  294.8 2.4 pad_maximum_fusion
  297.2 1.8 reshape.255
  299.0 10.4 %scatter_custom_fusion.1 = bf16[1024,2048]{1,0:T(8,128)(2,1)} fusion(s32[528]{0:T(1024)S(1)} %fusion.23, bf16[528,2048]{1,0:T(8,128)(2,1)} %reshape.255, bf16[]{:T(256)} %constant.66.clone.1), kind=kCustom, calls=%fused_computation.13 | custom fusion | bytes 4194816 | tf_op jit(solution)/shard_map/scatter | solution.py:73
  309.4 10.7 %all-to-all-start.2 = ((bf16[64,16,2048]{2,1,0:T(8,128)(2,1)}), bf16[64,16,2048]{2,1,0:T(8,128)(2,1)}, u32[]{:S(2)}, u32[]{:S(2)}) async-start(bf16[64,16,2048]{2,1,0:T(8,128)(2,1)} %bitcast.46), calls=%async_computation.3 | async-start | bytes 8388608 | tf_op jit(solution)/shard_map/all_to_all | solution.py:76
  320.9 0.7 reduce.10
  321.7 91.9 %all-to-all-done.2 = bf16[64,16,2048]{2,1,0:T(8,128)(2,1)} async-done(((bf16[64,16,2048]{2,1,0:T(8,128)(2,1)}), bf16[64,16,2048]{2,1,0:T(8,128)(2,1)}, u32[]{:S(2)}, u32[]{:S(2)}) %all-to-all-start.2) | async-done | bytes 4194336 | tf_op jit(solution)/shard_map/all_to_all | solution.py:76
  413.7 18.3 %scatter_custom_fusion.2 = f32[1024,2048]{1,0:T(8,128)} fusion(s32[1024]{0:T(1024)S(1)} %bitcast.56, bf16[1024,2048]{1,0:T(8,128)(2,1)} %bitcast.18, f32[]{:T(128)} %constant.69.clone.1), kind=kCustom, calls=%fused_computation.5 | custom fusion | flops 4194304 | bytes 12582916 | tf_op jit(solution)/shard_map/scatter-add | solution.py:78
  432.6 2.4 fusion.6
  434.9 0.9 fusion.3
  435.8 78.0 %reduce-scatter.5.cloned.1.call-done = f32[1024,512]{1,0:T(8,128)} async-done(((f32[1024,2048]{1,0:T(8,128)}), f32[1024,512]{1,0:T(8,128)}) %reduce-scatter.5.cloned.1.call-update) | async-done | bytes 2097168 | tf_op jit(solution)/shard_map/reduce_scatter | solution.py:81
  (39 shorter events, 3.2 us)
Async XLA Ops:
  7.2 57.1 %all-gather.4.cloned.1.call-start = ((), (), s32[]{:S(2)}) async-start(), calls=%async_computation.5 | async-start | bytes 5242880 | tf_op jit(solution)/shard_map/all_gather | solution.py:26
  80.3 104.6 %all-to-all-start.1 = ((bf16[64,16,2048]{2,1,0:T(8,128)(2,1)}), bf16[64,16,2048]{2,1,0:T(8,128)(2,1)}, u32[]{:S(2)}, u32[]{:S(2)}) async-start(bf16[64,16,2048]{2,1,0:T(8,128)(2,1)} %broadcast_select_fusion), calls=%async_computation.1 | async-start | bytes 8388608 | tf_op jit(solution)/shard_map/all_to_all | solution.py:29
  91.3 143.0 %all-gather.6.cloned.1.call-start = ((), (), s32[]{:S(2)}) async-start(), calls=%async_computation.8 | async-start | bytes 1114112 | tf_op jit(solution)/shard_map/all_gather | solution.py:34
  193.9 3.9 copy-start.1
  197.6 96.2 %reduce-scatter.3.cloned.1.call-start = ((), (), s32[]{:S(2)}) async-start(), calls=%async_computation.6 | async-start | bytes 2228224 | tf_op jit(solution)/shard_map/reduce_scatter | solution.py:64
  309.4 104.3 %all-to-all-start.2 = ((bf16[64,16,2048]{2,1,0:T(8,128)(2,1)}), bf16[64,16,2048]{2,1,0:T(8,128)(2,1)}, u32[]{:S(2)}, u32[]{:S(2)}) async-start(bf16[64,16,2048]{2,1,0:T(8,128)(2,1)} %bitcast.46), calls=%async_computation.3 | async-start | bytes 8388608 | tf_op jit(solution)/shard_map/all_to_all | solution.py:76
  320.1 193.7 %reduce-scatter.5.cloned.1.call-start = ((), (), s32[]{:S(2)}) async-start(), calls=%async_computation.7 | async-start | bytes 10485760 | tf_op jit(solution)/shard_map/reduce_scatter | solution.py:81
  432.0 2.9 copy-start
Sparse Core Ops, SparseCore 0:
  9.8 54.3 all-gather.3
  197.7 36.6 all-gather.5
  238.3 55.4 reduce-scatter.2
  432.2 81.6 reduce-scatter.4
where the time goes:
time: 521 us; the launch traced here: 520 us
  waiting for transfers between devices  378 us (73%)
  local copies, waits for them, and re-layouts  42.5 us (8%)
  other arithmetic  32.2 us (6%)
  starting transfers between devices  22.3 us (4%)
  blocking collectives  22 us (4%)
  between operations  14 us (3%)
  matrix products  9.2 us (2%)
    all_to_all x1, waiting for transfers between devices, body(): lax.all_to_all(found, ('dp', 'corpus'), split_axis=0, concat_axis=0, tile...  93.5 us
    all_to_all x1, waiting for transfers between devices, body(): lax.all_to_all(grad_slots, ('dp', 'corpus'), split_axis=0, concat_axis=0,...  91.9 us
    reduce_scatter x1, waiting for transfers between devices, body(): lax.psum_scatter(accum_grad, 'tensor', scatter_dimension=1, tiled=True)  78 us
    reduce_scatter x1, waiting for transfers between devices, body(): lax.psum_scatter(in_terms, 'dp', scatter_dimension=0, tiled=True)  53.7 us
    all_gather x1, waiting for transfers between devices, body(): in_batch = lax.all_gather(pos_rows, 'dp', axis=0, tiled=True)  34 us
    all_gather x1, waiting for transfers between devices, body(): row_table = lax.all_gather(passages, 'tensor', axis=1, tiled=True)  26.3 us
    all_to_all x1, blocking collectives, body(): lax.all_to_all(send_ids, ('dp', 'corpus'), split_axis=0, concat_axis=0, t...  22 us
    scatter-add x1, other arithmetic, body(): accum_grad.at[asked_ids.reshape(-1)]  18.3 us
  transfers between devices with their start and end apart: 6, of which 6 were waited for; matrix products, arithmetic and copies ran while one was open for 3% of the time, Pallas kernels for 0%

commit v1 on v0

--- a/solution.py
+++ b/solution.py
@@ -2,6 +2,28 @@
 import jax.numpy as jnp
 from jax import lax
 from jax.sharding import PartitionSpec as P
+
+
+def joined_along(parts, dim):
+    parts = jnp.moveaxis(parts, 0, dim)
+    lengths = parts.shape
+    return parts.reshape(*lengths[:dim], lengths[dim] * lengths[dim + 1], *lengths[dim + 2 :])
+
+
+def ring_gather(value, axis, dim):
+    devices = lax.axis_size(axis)
+    pairs = [(i, (i + 1) % devices) for i in range(devices)]
+    back = [(b, a) for a, b in pairs]
+    lower, upper = ([], [])
+    for step in range(devices - 1):
+        if step % 2 == 0:
+            lower.append(lax.ppermute(lower[-1] if lower else value, axis, pairs))
+        else:
+            upper.append(lax.ppermute(upper[-1] if upper else value, axis, back))
+    blocks = jnp.stack([*lower[::-1], value, *upper])
+    shift = lax.axis_index(axis) - len(lower)
+    blocks = blocks[(jnp.arange(devices) - shift) % devices]
+    return joined_along(blocks, dim)
 
 
 def lookup_rows(row_table, asked_ids):
@@ -23,7 +45,7 @@
     slot_of = owner_of * slot_count + jnp.sum(earlier * matches, axis=1)
     send_ids = jnp.full((owners * slot_count,), block_rows, jnp.int32).at[slot_of].set(local_row)
     send_ids = send_ids.reshape(owners, slot_count)
-    row_table = lax.all_gather(passages, "tensor", axis=1, tiled=True)
+    row_table = ring_gather(passages, "tensor", 1)
     asked_ids = lax.all_to_all(send_ids, ("dp", "corpus"), split_axis=0, concat_axis=0, tiled=True)
     found = lookup_rows(row_table, asked_ids)
     fetched = lax.all_to_all(found, ("dp", "corpus"), split_axis=0, concat_axis=0, tiled=True)

time: 521 us -> 530 us (1.017)
  blocking collectives: 22 us -> 0 us
  starting transfers between devices: 22.3 us -> 40.9 us
  local copies, waits for them, and re-layouts: 42.5 us -> 52.9 us
    all_gather x1 -> x0, waiting for transfers between devices: 26.3 us -> none  [body(): row_table = lax.all_gather(passages, 'tensor', axis=1, tiled=True)]
    all_to_all x1 -> x0, blocking collectives: 22 us -> none  [body(): lax.all_to_all(send_ids, ('dp', 'corpus'), split_axis=0, concat_axis=0, t...]
    ppermute x0 -> x3, waiting for transfers between devices: none -> 17.5 us  [the longest x2 17.5 us: ring_gather(): lower.append(lax.ppermute(lower[-1] if lower else value, axis, pairs))]
    all_to_all x0 -> x1, starting transfers between devices: none -> 13.4 us  [body(): lax.all_to_all(send_ids, ('dp', 'corpus'), split_axis=0, concat_axis=0, t...]
    all_to_all x0 -> x1, waiting for transfers between devices: none -> 9.08 us  [body(): lax.all_to_all(send_ids, ('dp', 'corpus'), split_axis=0, concat_axis=0, t...]
  transfers between devices with their start and end apart: 6 -> 9, of which waited for: 6 -> 7; matrix products, arithmetic and copies ran while one was open for 3% -> 3% of each run, Pallas kernels for 0% -> 0%
where the time goes in v1:
time: 530 us; the launch traced here: 529 us
  waiting for transfers between devices  377 us (71%)
  local copies, waits for them, and re-layouts  52.9 us (10%)
  starting transfers between devices  40.9 us (8%)
  other arithmetic  35.5 us (7%)
  between operations  14 us (3%)
  matrix products  9.2 us (2%)
    all_to_all x1, waiting for transfers between devices, body(): lax.all_to_all(found, ('dp', 'corpus'), split_axis=0, concat_axis=0, tile...  93.3 us
    all_to_all x1, waiting for transfers between devices, body(): lax.all_to_all(grad_slots, ('dp', 'corpus'), split_axis=0, concat_axis=0,...  92.2 us
    reduce_scatter x1, waiting for transfers between devices, body(): lax.psum_scatter(accum_grad, 'tensor', scatter_dimension=1, tiled=True)  78 us
    reduce_scatter x1, waiting for transfers between devices, body(): lax.psum_scatter(in_terms, 'dp', scatter_dimension=0, tiled=True)  53.7 us
    all_gather x1, waiting for transfers between devices, body(): in_batch = lax.all_gather(pos_rows, 'dp', axis=0, tiled=True)  32.8 us
    scatter-add x1, other arithmetic, body(): accum_grad.at[asked_ids.reshape(-1)]  18.3 us
    ppermute x2, waiting for transfers between devices, ring_gather(): lower.append(lax.ppermute(lower[-1] if lower else value, axis, pairs))  17.5 us
    all_to_all x1, starting transfers between devices, body(): lax.all_to_all(send_ids, ('dp', 'corpus'), split_axis=0, concat_axis=0, t...  13.4 us
  transfers between devices with their start and end apart: 9, of which 7 were waited for; matrix products, arithmetic and copies ran while one was open for 3% of the time, Pallas kernels for 0%

profile of v1, /device:TPU:1, one launch (start us, length us, event | category | flops | bytes accessed | tf_op | source)
XLA Modules:
  0.0 529.1 jit_solution(5606218844857086565)
XLA Ops:
  7.2 2.2 collective-permute-start
  9.4 1.5 collective-permute-start.2
  12.6 1.5 reduce-window.6
  14.5 17.5 %collective-permute-done = bf16[1024,512]{1,0:T(8,128)(2,1)S(1)} collective-permute-done((bf16[1024,512]{1,0:T(8,128)(2,1)}, bf16[1024,512]{1,0:T(8,128)(2,1)S(1)}, u32[]{:S(2)}, u32[]{:S(2)}) %collective-permute-start) | collective-permute-done | bytes 1048608 | tf_op jit(solution)/shard_map/ppermute | solution.py:20
  31.9 1.5 collective-permute-start.1
  33.6 4.1 scatter_custom_fusion
  38.4 13.4 %all-to-all-start = ((s32[64,1,16]{2,1,0:T(1,128)}), s32[64,1,16]{2,1,0:T(1,128)S(1)}, u32[]{:S(2)}, u32[]{:S(2)}) async-start(s32[64,1,16]{2,1,0:T(1,128)} %bitcast.2), calls=%async_computation | async-start | bytes 65536 | tf_op jit(solution)/shard_map/all_to_all | solution.py:49
  51.9 9.1 %all-to-all-done = s32[64,1,16]{2,1,0:T(1,128)S(1)} async-done(((s32[64,1,16]{2,1,0:T(1,128)}), s32[64,1,16]{2,1,0:T(1,128)S(1)}, u32[]{:S(2)}, u32[]{:S(2)}) %all-to-all-start) | async-done | bytes 4128 | tf_op jit(solution)/shard_map/all_to_all | solution.py:49
  61.1 3.3 pad_maximum_fusion
  64.4 4.9 gather_fusion
  69.3 4.8 copy.28
  74.1 11.6 %gather_fusion.1 = bf16[1024,2048]{1,0:T(8,128)(2,1)} fusion(bf16[1024,2048]{1,0:T(8,128)(2,1)} %bitcast.55, s32[1024]{0:T(1024)S(1)} %broadcast_clamp_fusion), kind=kCustom, calls=%fused_computation.1 | custom fusion | bytes 8392704 | tf_op jit(solution)/shard_map/jit(_take)/gather | solution.py:30
  85.7 4.5 broadcast_select_fusion
  90.2 11.0 %all-to-all-start.1 = ((bf16[64,16,2048]{2,1,0:T(8,128)(2,1)}), bf16[64,16,2048]{2,1,0:T(8,128)(2,1)}, u32[]{:S(2)}, u32[]{:S(2)}) async-start(bf16[64,16,2048]{2,1,0:T(8,128)(2,1)} %broadcast_select_fusion), calls=%async_computation.1 | async-start | bytes 8388608 | tf_op jit(solution)/shard_map/all_to_all | solution.py:51
  101.4 93.3 %all-to-all-done.1 = bf16[64,16,2048]{2,1,0:T(8,128)(2,1)} async-done(((bf16[64,16,2048]{2,1,0:T(8,128)(2,1)}), bf16[64,16,2048]{2,1,0:T(8,128)(2,1)}, u32[]{:S(2)}, u32[]{:S(2)}) %all-to-all-start.1) | async-done | bytes 4194336 | tf_op jit(solution)/shard_map/all_to_all | solution.py:51
  194.7 9.0 %gather_fusion.2 = bf16[528,2048]{1,0:T(8,128)(2,1)S(1)} fusion(bf16[1024,2048]{1,0:T(8,128)(2,1)} %bitcast.12, s32[1024]{0:T(1024)S(1)} %pad_clamp_fusion), kind=kCustom, calls=%fused_computation.2 | custom fusion | bytes 4327488 | tf_op jit(solution)/shard_map/gather | solution.py:52
  203.8 1.9 reshape.275
  205.6 1.1 slice.36
  207.5 2.4 fusion.8
  210.1 32.8 %all-gather.3.cloned.1.call-done = bf16[256,1,2048]{2,0,1:T(8,128)(2,1)} async-done(((bf16[16,1,2048]{2,0,1:T(8,128)(2,1)}), bf16[256,1,2048]{2,0,1:T(8,128)(2,1)}) %all-gather.3.cloned.1.call-update) | async-done | bytes 1048592 | tf_op jit(solution)/shard_map/all_gather | solution.py:56
  242.8 1.7 fusion.29
  244.8 1.8 fusion.18
  246.7 1.8 multiply_convert_fusion
  248.5 53.7 %reduce-scatter.3.cloned.1.call-done = f32[16,2048]{1,0:T(8,128)} async-done(((f32[256,2048]{1,0:T(8,128)}), f32[16,2048]{1,0:T(8,128)}) %reduce-scatter.3.cloned.1.call-update) | async-done | bytes 131088 | tf_op jit(solution)/shard_map/reduce_scatter | solution.py:86
  303.3 2.4 pad_maximum_fusion.1
  305.7 1.8 reshape.316
  307.4 10.4 %scatter_custom_fusion.1 = bf16[1024,2048]{1,0:T(8,128)(2,1)} fusion(s32[528]{0:T(1024)S(1)} %fusion.23, bf16[528,2048]{1,0:T(8,128)(2,1)} %reshape.316, bf16[]{:T(256)} %constant.90.clone.1), kind=kCustom, calls=%fused_computation.15 | custom fusion | bytes 4194816 | tf_op jit(solution)/shard_map/scatter | solution.py:95
  317.8 11.0 %all-to-all-start.2 = ((bf16[64,16,2048]{2,1,0:T(8,128)(2,1)}), bf16[64,16,2048]{2,1,0:T(8,128)(2,1)}, u32[]{:S(2)}, u32[]{:S(2)}) async-start(bf16[64,16,2048]{2,1,0:T(8,128)(2,1)} %bitcast.56), calls=%async_computation.3 | async-start | bytes 8388608 | tf_op jit(solution)/shard_map/all_to_all | solution.py:98
  330.2 92.2 %all-to-all-done.2 = bf16[64,16,2048]{2,1,0:T(8,128)(2,1)} async-done(((bf16[64,16,2048]{2,1,0:T(8,128)(2,1)}), bf16[64,16,2048]{2,1,0:T(8,128)(2,1)}, u32[]{:S(2)}, u32[]{:S(2)}) %all-to-all-start.2) | async-done | bytes 4194336 | tf_op jit(solution)/shard_map/all_to_all | solution.py:98
  422.3 18.3 %scatter_custom_fusion.2 = f32[1024,2048]{1,0:T(8,128)} fusion(s32[1024]{0:T(1024)S(1)} %bitcast.70, bf16[1024,2048]{1,0:T(8,128)(2,1)} %bitcast.24, f32[]{:T(128)} %constant.93.clone.1), kind=kCustom, calls=%fused_computation.6 | custom fusion | flops 4194304 | bytes 12582916 | tf_op jit(solution)/shard_map/scatter-add | solution.py:100
  441.2 2.4 fusion.6
  444.5 78.0 %reduce-scatter.5.cloned.1.call-done = f32[1024,512]{1,0:T(8,128)} async-done(((f32[1024,2048]{1,0:T(8,128)}), f32[1024,512]{1,0:T(8,128)}) %reduce-scatter.5.cloned.1.call-update) | async-done | bytes 2097168 | tf_op jit(solution)/shard_map/reduce_scatter | solution.py:103
  (48 shorter events, 8.3 us)
Async XLA Ops:
  7.2 24.8 %collective-permute-start = (bf16[1024,512]{1,0:T(8,128)(2,1)}, bf16[1024,512]{1,0:T(8,128)(2,1)S(1)}, u32[]{:S(2)}, u32[]{:S(2)}) collective-permute-start(bf16[1024,512]{1,0:T(8,128)(2,1)} %param.5), channel_id=1, source_target_pairs={{0,4},{4,8},{8,12},{12,0},{1,5},{5,9},{9,13},{13,1},{2,6},{6,10},{... | collective-permute-start | bytes 3145736 | tf_op jit(solution)/shard_map/ppermute | solution.py:20
  9.4 51.8 %collective-permute-start.2 = (bf16[1024,512]{1,0:T(8,128)(2,1)}, bf16[1024,512]{1,0:T(8,128)(2,1)S(1)}, u32[]{:S(2)}, u32[]{:S(2)}) collective-permute-start(bf16[1024,512]{1,0:T(8,128)(2,1)} %param.5), channel_id=1, source_target_pairs={{4,0},{8,4},{12,8},{0,12},{5,1},{9,5},{13,9},{1,13},{6,2},{10,6},{... | collective-permute-start | bytes 3145736 | tf_op jit(solution)/shard_map/ppermute | solution.py:22
  31.9 29.2 %collective-permute-start.1 = (bf16[1024,512]{1,0:T(8,128)(2,1)S(1)}, bf16[1024,512]{1,0:T(8,128)(2,1)S(1)}, u32[]{:S(2)}, u32[]{:S(2)}) collective-permute-start(bf16[1024,512]{1,0:T(8,128)(2,1)S(1)} %collective-permute-done), channel_id=1, source_target_pairs={{0,4},{4,8},{8,12},{12,0},{1,5},{5,9},{9,13},{13,1},{2,6},{6,10},{... | collective-permute-start | bytes 3145736 | tf_op jit(solution)/shard_map/ppermute | solution.py:20
  38.4 22.6 %all-to-all-start = ((s32[64,1,16]{2,1,0:T(1,128)}), s32[64,1,16]{2,1,0:T(1,128)S(1)}, u32[]{:S(2)}, u32[]{:S(2)}) async-start(s32[64,1,16]{2,1,0:T(1,128)} %bitcast.2), calls=%async_computation | async-start | bytes 65536 | tf_op jit(solution)/shard_map/all_to_all | solution.py:49
  90.2 104.5 %all-to-all-start.1 = ((bf16[64,16,2048]{2,1,0:T(8,128)(2,1)}), bf16[64,16,2048]{2,1,0:T(8,128)(2,1)}, u32[]{:S(2)}, u32[]{:S(2)}) async-start(bf16[64,16,2048]{2,1,0:T(8,128)(2,1)} %broadcast_select_fusion), calls=%async_computation.1 | async-start | bytes 8388608 | tf_op jit(solution)/shard_map/all_to_all | solution.py:51
  101.2 141.6 %all-gather.3.cloned.1.call-start = ((), (), s32[]{:S(2)}) async-start(), calls=%async_computation.7 | async-start | bytes 1114112 | tf_op jit(solution)/shard_map/all_gather | solution.py:56
  203.8 3.8 copy-start.1
  207.5 94.8 %reduce-scatter.3.cloned.1.call-start = ((), (), s32[]{:S(2)}) async-start(), calls=%async_computation.5 | async-start | bytes 2228224 | tf_op jit(solution)/shard_map/reduce_scatter | solution.py:86
  317.8 104.5 %all-to-all-start.2 = ((bf16[64,16,2048]{2,1,0:T(8,128)(2,1)}), bf16[64,16,2048]{2,1,0:T(8,128)(2,1)}, u32[]{:S(2)}, u32[]{:S(2)}) async-start(bf16[64,16,2048]{2,1,0:T(8,128)(2,1)} %bitcast.56), calls=%async_computation.3 | async-start | bytes 8388608 | tf_op jit(solution)/shard_map/all_to_all | solution.py:98
  328.8 193.7 %reduce-scatter.5.cloned.1.call-start = ((), (), s32[]{:S(2)}) async-start(), calls=%async_computation.6 | async-start | bytes 10485760 | tf_op jit(solution)/shard_map/reduce_scatter | solution.py:103
  440.7 2.9 copy-start
Sparse Core Ops, SparseCore 0:
  207.6 35.1 all-gather.2
  246.8 55.3 reduce-scatter.2
  440.8 81.6 reduce-scatter.4
